TPU v7x, 256 devices: a whole 4x4x8 slice. The times are simulated.
256 devices in a mesh: gx: 16 (over x_lo, z), gz: 16 (over y, x_hi, core).
Axes of the slice: x: 4 (x_hi: 2, x_lo: 2; x = x_hi * 2 + x_lo), y: 4, z: 8, core: 2. Of those that a mesh axis runs over, the one named last changes fastest.
Arguments:
- conserved_fields: float32 [6, 256, 512, 128], P(None, 'gx', 'gz'), may hold values from -2 to 62, as said below
- coeff: bfloat16 [2, 1024, 6, 128, 512], P(None, 'gx', None, 'gz'), may hold values from -0.25 to 0.25
- feed_plane: int32 [25], replicated, may hold values from 0 to 2047
Outputs:
- new_state: float32 [6, 256, 512, 128], P(None, 'gx', 'gz')
Inputs may be any that keep to these rules, and one draw needn't show every extreme that they name: `conserved_fields`: each cell is the conserved form of a gas with density 0.5 to 2, temperature 0.5 to 2, streamwise velocity -1 to 7, wall-normal and spanwise velocities -1 to 1 and vibrational energy per unit mass 0.05 to 0.5.
All inputs are finite; a program needn't handle non-finite values.
Results may differ from a plain program's by a relative error of at most 0.00038.
Values sent between devices are 32-bit elements; how exact they have to be, the bound alone decides.
A program may use at most 192 MiB of HBM per device.

v0:
```python
import math

import jax
import jax.numpy as jnp
from jax import lax
from jax.sharding import PartitionSpec as P

ADIABATIC_INDEX = 1.4
CAPACITY_CONST = 2.5
OSCILLATOR_SCALE = 2.0
VIBRANT_LAG = 0.5
LANDAU_FIT_LAW = 1.5
SURFACE_DIST_SQ = 0.36
TIME_STEP = 0.05
FORCING_RATE = 2.0
WENO_EPSILON = 1e-06


def cut_along(x, dim, devices):
    before, after = (x.shape[:dim], x.shape[dim + 1 :])
    return jnp.moveaxis(x.reshape(*before, devices, -1, *after), dim, 0)


def summed_on_arrival(x, axis, dim):
    devices = lax.axis_size(axis)
    tiles = lax.all_to_all(cut_along(x, dim, devices), axis, 0, 0, tiled=True)
    return jnp.sum(tiles, axis=0)


def with_halo(x, sides, width):
    for axis, dim in sides:
        devices, length = (lax.axis_size(axis), x.shape[dim])
        up = [(i, (i + 1) % devices) for i in range(devices)]
        down = [(j, i) for i, j in up]
        last = lax.slice_in_dim(x, length - width, length, axis=dim)
        leading = lax.slice_in_dim(x, 0, width, axis=dim)
        before = lax.ppermute(last, axis, up)
        after = lax.ppermute(leading, axis, down)
        x = jnp.concatenate([before, x, after], axis=dim)
    return x


def caloric_bundle(conserved_fields):
    fluid_rho_field = conserved_fields[0]
    motion_share = (
        0.5
        * (
            jnp.square(conserved_fields[1])
            + jnp.square(conserved_fields[2])
            + jnp.square(conserved_fields[3])
        )
        / jnp.square(fluid_rho_field)
    )
    translational_kelvin = (
        conserved_fields[4] / fluid_rho_field - motion_share - conserved_fields[5] / fluid_rho_field
    ) / CAPACITY_CONST
    thermodynamic_stress = fluid_rho_field * translational_kelvin
    return (fluid_rho_field, translational_kelvin, thermodynamic_stress)


def directional(extended_fields, component):
    fluid_rho_field, translational_kelvin, thermodynamic_stress = caloric_bundle(extended_fields)
    crossflow_flux_field = extended_fields[component] / fluid_rho_field
    flux_rows = []
    for member in range(6):
        entry = extended_fields[member] * crossflow_flux_field
        if member == component:
            entry = entry + thermodynamic_stress
        if member == 4:
            entry = entry + thermodynamic_stress * crossflow_flux_field
        flux_rows.append(entry)
    forcing_samples = jnp.abs(crossflow_flux_field) + jnp.sqrt(
        ADIABATIC_INDEX * translational_kelvin
    )
    return (jnp.stack(flux_rows), forcing_samples)


def weno_face(minus_two, minus_one, centre, plus_one, plus_two):
    low_poly = (2.0 * minus_two - 7.0 * minus_one + 11.0 * centre) / 6.0
    mid_poly = (-minus_one + 5.0 * centre + 2.0 * plus_one) / 6.0
    high_poly = (2.0 * centre + 5.0 * plus_one - plus_two) / 6.0
    low_beta = 13.0 / 12.0 * jnp.square(minus_two - 2.0 * minus_one + centre) + 0.25 * jnp.square(
        minus_two - 4.0 * minus_one + 3.0 * centre
    )
    mid_beta = 13.0 / 12.0 * jnp.square(minus_one - 2.0 * centre + plus_one) + 0.25 * jnp.square(
        minus_one - plus_one
    )
    high_beta = 13.0 / 12.0 * jnp.square(centre - 2.0 * plus_one + plus_two) + 0.25 * jnp.square(
        3.0 * centre - 4.0 * plus_one + plus_two
    )
    low_weight = 0.1 / jnp.square(WENO_EPSILON + low_beta)
    mid_weight = 0.6 / jnp.square(WENO_EPSILON + mid_beta)
    high_weight = 0.3 / jnp.square(WENO_EPSILON + high_beta)
    return (low_weight * low_poly + mid_weight * mid_poly + high_weight * high_poly) / (
        low_weight + mid_weight + high_weight
    )


def sweep_axis(extended_fields, axis, component):
    length = extended_fields.shape[axis] - 6
    fluxes, forcing_samples = directional(extended_fields, component)

    def window(array, offset, dim):
        return lax.slice_in_dim(array, offset, offset + length + 1, axis=dim)

    wave_speed = window(forcing_samples, 0, axis - 1)
    for offset in range(1, 6):
        wave_speed = jnp.maximum(wave_speed, window(forcing_samples, offset, axis - 1))
    wave_speed = wave_speed[None]
    upwind = [
        0.5 * (window(fluxes, offset, axis) + wave_speed * window(extended_fields, offset, axis))
        for offset in range(5)
    ]
    downwind = [
        0.5 * (window(fluxes, offset, axis) - wave_speed * window(extended_fields, offset, axis))
        for offset in (5, 4, 3, 2, 1)
    ]
    face_flux = weno_face(*upwind) + weno_face(*downwind)
    return lax.slice_in_dim(face_flux, 1, length + 1, axis=axis) - lax.slice_in_dim(
        face_flux, 0, length, axis=axis
    )


def wall_pad(conserved_fields):
    reflected_fields = conserved_fields[:, :, :, 2::-1]
    translational_kelvin = caloric_bundle(reflected_fields)[1]
    ghost_layer_kelvin = SURFACE_DIST_SQ / translational_kelvin
    ghost_layer_oscillator = reflected_fields[4] - CAPACITY_CONST * reflected_fields[0] * (
        translational_kelvin - ghost_layer_kelvin
    )
    ghost_cells = jnp.stack(
        [
            reflected_fields[0],
            -reflected_fields[1],
            -reflected_fields[2],
            -reflected_fields[3],
            ghost_layer_oscillator,
            reflected_fields[5],
        ]
    )
    top_cells = jnp.repeat(conserved_fields[:, :, :, -1:], 3, axis=3)
    return jnp.concatenate([ghost_cells, conserved_fields, top_cells], axis=3)


def relaxation(conserved_fields):
    fluid_rho_field, translational_kelvin, thermodynamic_stress = caloric_bundle(conserved_fields)
    balanced_oscillator_share = OSCILLATOR_SCALE / (
        jnp.exp(OSCILLATOR_SCALE / translational_kelvin) - 1.0
    )
    settling_interval = (
        VIBRANT_LAG
        * jnp.exp(LANDAU_FIT_LAW * (jnp.exp(-jnp.log(translational_kelvin) / 3.0) - 1.0))
        / thermodynamic_stress
    )
    return (fluid_rho_field * balanced_oscillator_share - conserved_fields[5]) / settling_interval


def local(conserved_fields, coeff, feed_plane):
    groups_x = lax.axis_size("gx")
    groups_z = lax.axis_size("gz")
    plane_count = conserved_fields.shape[1]
    span_cells = conserved_fields.shape[2]
    span_total = span_cells * groups_z
    kx_local = coeff.shape[1]
    levels_local = coeff.shape[3]
    span_modes = coeff.shape[4]
    stream_points = 2 * kx_local * groups_x
    planes = feed_plane.shape[0]
    span_ids = (
        jnp.arange(span_modes, dtype=jnp.int32)[:, None]
        * jnp.arange(span_total, dtype=jnp.int32)[None, :]
        % span_modes
    )
    span_angle = 2.0 * math.pi / span_modes * span_ids.astype(jnp.float32)
    span_table = jnp.concatenate([jnp.cos(span_angle), jnp.sin(span_angle)], axis=1).astype(
        jnp.bfloat16
    )
    mode_ids = lax.axis_index("gx") * kx_local + jnp.arange(kx_local, dtype=jnp.int32)
    stream_ids = feed_plane[:, None] * mode_ids[None, :] % stream_points
    stream_angle = 2.0 * math.pi / stream_points * stream_ids.astype(jnp.float32)
    stream_table = jnp.concatenate([jnp.cos(stream_angle), -jnp.sin(stream_angle)], axis=1).astype(
        jnp.bfloat16
    )
    coeff_rows = coeff.reshape(2 * kx_local * 6 * levels_local, span_modes)
    product = jnp.dot(coeff_rows, span_table, preferred_element_type=jnp.float32)
    product = product.reshape(2, kx_local, 6, levels_local, 2 * span_total)
    real_part = product[0, :, :, :, :span_total] - product[1, :, :, :, span_total:]
    imag_part = product[0, :, :, :, span_total:] + product[1, :, :, :, :span_total]
    mixed_modes = jnp.concatenate([real_part, imag_part], axis=0).astype(jnp.bfloat16)
    row_block = (6 * planes + groups_x - 1) // groups_x
    total_rows = row_block * groups_x
    table_rows = total_rows // 6 + 3
    padded_table = jnp.concatenate(
        [stream_table, jnp.zeros((table_rows - planes, 2 * kx_local), jnp.bfloat16)], axis=0
    )
    modes_flat = mixed_modes.reshape(2 * kx_local, 6 * levels_local * span_total)
    start = jnp.int32(0)
    plane_span = row_block * lax.axis_size("gx") // 6 + 2
    first_plane = start // 6
    table_block = lax.dynamic_slice_in_dim(padded_table, first_plane, plane_span, 0)
    products = jnp.dot(table_block, modes_flat, preferred_element_type=jnp.float32)
    products = products.reshape(plane_span * 6, levels_local * span_total)
    reduced = summed_on_arrival(
        lax.dynamic_slice_in_dim(products, start, row_block * lax.axis_size("gx"), 0), "gx", 0
    )
    reduced = reduced.reshape(row_block, levels_local, span_total)
    relaid = lax.all_to_all(reduced, "gz", split_axis=2, concat_axis=1, tiled=True)
    collected = lax.all_gather(relaid, "gx", axis=0, tiled=True)
    feed_values = collected[: 6 * planes].reshape(planes, 6, levels_local * groups_z, span_cells)
    target = jnp.transpose(feed_values, (1, 0, 3, 2))
    stream_pad = with_halo(conserved_fields, (("gx", 1),), 3)
    span_pad = with_halo(conserved_fields, (("gz", 2),), 3)
    at_inlet = lax.axis_index("gx") == 0
    at_outlet = lax.axis_index("gx") == groups_x - 1
    lower = jnp.where(at_inlet, jnp.repeat(conserved_fields[:, :1], 3, axis=1), stream_pad[:, :3])
    upper = jnp.where(
        at_outlet, jnp.repeat(conserved_fields[:, -1:], 3, axis=1), stream_pad[:, -3:]
    )
    stream_pad = jnp.concatenate([lower, conserved_fields, upper], axis=1)
    tendency = -(
        sweep_axis(stream_pad, 1, 1)
        + sweep_axis(span_pad, 2, 3)
        + sweep_axis(wall_pad(conserved_fields), 3, 2)
    )
    tendency = tendency.at[5].add(relaxation(conserved_fields))
    plane_global = lax.axis_index("gx") * plane_count + jnp.arange(plane_count, dtype=jnp.int32)
    inside = plane_global < planes
    strength = jnp.where(
        inside, FORCING_RATE * jnp.square(1.0 - plane_global.astype(jnp.float32) / planes), 0.0
    )
    picked = jnp.take(target, jnp.minimum(plane_global, planes - 1), axis=1)
    tendency = tendency + strength[None, :, None, None] * (picked - conserved_fields)
    return conserved_fields + TIME_STEP * tendency


def solution(mesh):
    placed = (P(None, "gx", "gz", None), P(None, "gx", None, "gz", None), P())
    return jax.shard_map(
        local, mesh=mesh, in_specs=placed, out_specs=P(None, "gx", "gz", None), check_vma=False
    )
```

profile of v0, /device:TPU:8, one launch (start us, length us, event | category | flops | bytes accessed | tf_op | source)
XLA Modules:
  0.0 323.3 jit_solution(15336654425104593148)
XLA Ops:
  6.5 1.7 constant_dynamic-update-slice_fusion.1
  9.0 2.3 collective-permute-start.3
  12.3 5.9 %collective-permute-start.1 = (f32[6,3,32,128]{3,2,0,1:T(8,128)}, f32[6,3,32,128]{3,2,0,1:T(8,128)}, u32[]{:S(2)}, u32[]{:S(2)}) collective-permute-start(f32[6,3,32,128]{3,2,0,1:T(8,128)} %get-tuple-element.31), channel_id=1, source_target_pairs={{16,0},{32,16},{48,32},{64,48},{80,64},{96,80},{112,96},{128,112},... | collective-permute-start | bytes 884744 | tf_op jit(solution)/shard_map/ppermute | solution.py:38
  18.2 4.9 %sine_convert_fusion = (bf16[512,512]{1,0:T(8,128)(2,1)}, bf16[512,512]{1,0:T(8,128)(2,1)}) fusion(), kind=kLoop, calls=%fused_computation.114 | loop fusion | flops 4194304 | bytes 1048576 | tf_op jit(solution)/shard_map/convert.5
  23.1 14.0 %convolution_bitcast_fusion = f32[6144,1024]{0,1:T(8,128)} fusion(bf16[6144,512]{1,0:T(8,128)(2,1)} %bitcast.56, bf16[512,512]{1,0:T(8,128)(2,1)} %get-tuple-element.44, bf16[512,512]{1,0:T(8,128)(2,1)} %get-tuple-element.45), kind=kOutput, calls=%fused_computation.1 | convolution fusion | flops 6444548096 | bytes 32505856 | tf_op jit(solution)/shard_map/dot_general | solution.py:185
  37.1 24.7 %copy.173 = f32[6144,1024]{1,0:T(8,128)} copy(f32[6144,1024]{0,1:T(8,128)} %convolution_bitcast_fusion) | data formatting | bytes 50331648 | tf_op jit(solution)/shard_map/dot_general | solution.py:185
  61.9 12.3 %fusion.1 = (bf16[1,64,6,8,512]{4,3,2,1,0:T(8,128)(2,1)}, bf16[1,64,6,8,512]{4,3,2,1,0:T(8,128)(2,1)}) fusion(f32[2,64,6,8,1024]{4,3,2,1,0:T(8,128)} %bitcast.47), kind=kLoop, calls=%fused_computation.5 | loop fusion | flops 6291456 | bytes 31457280 | tf_op jit(solution)/shard_map/convert.3
  74.1 4.8 %add.739 = bf16[64,24576]{1,0:T(8,128)(2,1)} reshape(bf16[1,64,6,8,512]{4,3,2,1,0:T(8,128)(2,1)} %get-tuple-element.27) | data formatting | bytes 6291456 | tf_op jit(solution)/shard_map/add | solution.py:188
  79.0 4.8 %sub.382 = bf16[64,24576]{1,0:T(8,128)(2,1)} reshape(bf16[1,64,6,8,512]{4,3,2,1,0:T(8,128)(2,1)} %get-tuple-element.26) | data formatting | bytes 6291456 | tf_op jit(solution)/shard_map/sub | solution.py:187
  84.0 5.6 %fusion.2 = f32[28,24576]{1,0:T(8,128)} fusion(bf16[64,24576]{1,0:T(8,128)(2,1)} %add.739, bf16[64,24576]{1,0:T(8,128)(2,1)} %sub.382, bf16[25,64]{1,0:T(8,128)(2,1)S(1)} %get-tuple-element.43, bf16[25,64]{1,0:T(8,128)(2,1)S(1)} %get-tuple-element.42), kind=kOutput, calls=%fused_computation.6 | convolution fusion | flops 188772352 | bytes 9050368 | tf_op jit(solution)/shard_map/dot_general | solution.py:201
  89.5 3.3 %reshape.160 = f32[168,4096]{1,0:T(8,128)} reshape(f32[28,24576]{1,0:T(8,128)} %fusion.2) | data formatting | bytes 5505024 | tf_op jit(solution)/shard_map/reshape | solution.py:202
  92.8 3.5 %dynamic_slice.8 = f32[160,4096]{1,0:T(8,128)} slice(f32[168,4096]{1,0:T(8,128)} %reshape.160), slice={[0:160], [0:4096]} | slice | bytes 5242880 | tf_op jit(solution)/shard_map/dynamic_slice | solution.py:204
  96.3 3.5 %reshape.161 = f32[16,10,4096]{2,1,0:T(8,128)} reshape(f32[160,4096]{1,0:T(8,128)} %dynamic_slice.8) | data formatting | bytes 5242880 | tf_op jit(solution)/shard_map/reshape | solution.py:21
  99.8 5.6 %all-to-all-start = ((f32[16,10,4096]{2,1,0:T(8,128)}), f32[16,10,4096]{2,1,0:T(8,128)}, u32[]{:S(2)}, u32[]{:S(2)}) async-start(f32[16,10,4096]{2,1,0:T(8,128)} %reshape.161), calls=%async_computation | async-start | bytes 8388608 | tf_op jit(solution)/shard_map/all_to_all | solution.py:26
  105.4 3.1 slice.508
  110.4 2.8 copy.191
  113.3 1.7 copy.184
  116.3 1.7 copy.185
  118.1 1.7 copy.186
  119.8 1.7 copy.187
  121.5 1.7 copy.188
  123.2 1.7 copy.189
  129.0 1.5 constant_dynamic-update-slice_fusion.3
  130.5 1.4 constant_dynamic-update-slice_fusion.2
  131.8 2.7 copy.162
  134.5 1.4 reshape.157
  135.9 1.4 pad_maximum_fusion.2
  139.4 19.7 %divide_add_fusion = f32[6,16,32,129]{3,2,0,1:T(8,128)} fusion(f32[6,16,32,3]{3,2,0,1:T(8,128)S(1)} %reshape.157, f32[6,16,32,128]{3,2,0,1:T(8,128)S(1)} %get-tuple-element.35, f32[6,16,32,134]{3,2,0,1:T(8,128)S(1)} %multiply_dynamic-update-slice_fusion.1, f32[6,16,32,3]{3,2,0,1:T(8,128)S(1)} %copy-done.4, f32[16,32,129]{2,1,0:T(8,128)S(1)} %slice_maximum_fusion), kind=kLoop, calls=%fused_computation.33 | loop fusion | flops 60632064 | bytes 13006848 | tf_op jit(solution)/shard_map/add | solution.py:118
  162.2 13.0 %divide_add_fusion.1 = f32[6,16,33,128]{3,2,0,1:T(8,128)} fusion(f32[6,16,35,128]{3,2,0,1:T(8,128)S(1)} %constant_dynamic-update-slice_fusion, f32[6,16,38,128]{3,2,0,1:T(8,128)S(1)} %multiply_dynamic-update-slice_fusion.11, f32[6,16,32,128]{3,2,0,1:T(8,128)S(1)} %get-tuple-element.35, f32[6,16,3,128]{3,2,0,1:T(4,128)} %collective-permute-done.2, ...), kind=kLoop, calls=%fused_computation.62 | loop fusion | flops 60825600 | bytes 18210816 | tf_op jit(solution)/shard_map/add | solution.py:118
  179.5 22.3 %all-to-all-done = f32[16,10,4096]{2,1,0:T(8,128)} async-done(((f32[16,10,4096]{2,1,0:T(8,128)}), f32[16,10,4096]{2,1,0:T(8,128)}, u32[]{:S(2)}, u32[]{:S(2)}) %all-to-all-start) | async-done | bytes 2621472 | tf_op jit(solution)/shard_map/all_to_all | solution.py:26
  201.9 2.4 reduce_sum.9
  204.5 2.0 copy.174
  206.6 4.0 %reshape.206 = f32[16,1,2560]{2,1,0:T(1,128)} reshape(f32[512,8,10]{2,1,0:T(8,128)} %bitcast.49) | data formatting | bytes 327680
  210.6 6.0 %all-to-all-start.1 = ((f32[16,1,2560]{2,1,0:T(1,128)}), f32[16,1,2560]{2,1,0:T(1,128)S(1)}, u32[]{:S(2)}, u32[]{:S(2)}) async-start(f32[16,1,2560]{2,1,0:T(1,128)} %reshape.206), calls=%async_computation.1 | async-start | bytes 327680 | tf_op jit(solution)/shard_map/all_to_all | solution.py:207
  217.4 5.6 %all-to-all-done.1 = f32[16,1,2560]{2,1,0:T(1,128)S(1)} async-done(((f32[16,1,2560]{2,1,0:T(1,128)}), f32[16,1,2560]{2,1,0:T(1,128)S(1)}, u32[]{:S(2)}, u32[]{:S(2)}) %all-to-all-start.1) | async-done | bytes 163872 | tf_op jit(solution)/shard_map/all_to_all | solution.py:207
  224.6 3.6 %reshape.207 = f32[512,8,10]{2,1,0:T(8,128)} reshape(f32[16,2560]{1,0:T(8,128)S(1)} %reduce.2) | data formatting | bytes 327680
  228.1 3.3 %copy.176 = f32[10,16,8,32]{3,2,1,0:T(8,128)} copy(f32[10,16,8,32]{0,2,3,1:T(8,128)} %bitcast.50) | data formatting | bytes 327680 | tf_op jit(solution)/shard_map/all_to_all | solution.py:207
  231.5 2.0 copy.177
  233.5 2.2 add_dynamic-update-slice_fusion.1
  235.6 1.8 multiply_dynamic-update-slice_fusion.8
  240.0 11.2 %divide_add_fusion.2 = f32[6,17,32,128]{3,2,0,1:T(8,128)S(1)} fusion(f32[6,3,32,128]{3,2,0,1:T(8,128)S(1)} %broadcast_select_fusion, f32[6,16,32,128]{3,2,0,1:T(8,128)S(1)} %get-tuple-element.35, f32[6,22,32,128]{3,2,0,1:T(8,128)} %multiply_dynamic-update-slice_fusion.6, f32[6,3,32,128]{3,2,0,1:T(8,128)S(1)} %copy-done.8, f32[17,32,128]{2,1,0:T(8,128)S(1)} %copy-done.9), kind=kLoop, calls=%fused_computation.87 | loop fusion | flops 63922176 | bytes 14139392 | tf_op jit(solution)/shard_map/add | solution.py:118
  251.3 1.9 fusion.47
  253.2 2.0 fusion.70
  255.2 50.4 %all-gather.2.cloned.1.call-done = f32[160,128,32]{1,2,0:T(8,128)} async-done(((f32[10,128,32]{1,2,0:T(8,128)}), f32[160,128,32]{1,2,0:T(8,128)}) %all-gather.2.cloned.1.call-update) | async-done | bytes 2621456 | tf_op jit(solution)/shard_map/all_gather | solution.py:208
  305.6 1.7 slice-done
  307.3 1.7 copy.197
  309.0 3.6 %gather_fusion = f32[16,6,32,128]{3,2,1,0:T(8,128)} fusion(f32[6,25,32,128]{3,2,1,0:T(8,128)} %bitcast.51, s32[1024]{0:T(1024)S(1)} %pad_clamp_fusion), kind=kCustom, calls=%fused_computation | custom fusion | bytes 3145792 | tf_op jit(solution)/shard_map/jit(_take)/gather | solution.py:231
  312.6 2.5 fusion.52
  (81 shorter events, 24.9 us)
Async XLA Ops:
  9.0 150.0 %collective-permute-start.3 = (f32[6,16,3,128]{3,2,0,1:T(4,128)}, f32[6,16,3,128]{3,2,0,1:T(4,128)}, u32[]{:S(2)}, u32[]{:S(2)}) collective-permute-start(f32[6,16,3,128]{3,2,0,1:T(4,128)} %get-tuple-element.33), channel_id=1, source_target_pairs={{1,0},{2,1},{3,2},{4,3},{5,4},{6,5},{7,6},{8,7},{9,8},{10,9},{11,1... | collective-permute-start | bytes 442376 | tf_op jit(solution)/shard_map/ppermute | solution.py:38
  11.4 147.7 %collective-permute-start.2 = (f32[6,16,3,128]{3,2,0,1:T(4,128)}, f32[6,16,3,128]{3,2,0,1:T(4,128)}, u32[]{:S(2)}, u32[]{:S(2)}) collective-permute-start(f32[6,16,3,128]{3,2,0,1:T(4,128)} %get-tuple-element.32), channel_id=1, source_target_pairs={{0,1},{1,2},{2,3},{3,4},{4,5},{5,6},{6,7},{7,8},{8,9},{9,10},{10,1... | collective-permute-start | bytes 442376 | tf_op jit(solution)/shard_map/ppermute | solution.py:37
  12.3 163.0 %collective-permute-start.1 = (f32[6,3,32,128]{3,2,0,1:T(8,128)}, f32[6,3,32,128]{3,2,0,1:T(8,128)}, u32[]{:S(2)}, u32[]{:S(2)}) collective-permute-start(f32[6,3,32,128]{3,2,0,1:T(8,128)} %get-tuple-element.31), channel_id=1, source_target_pairs={{16,0},{32,16},{48,32},{64,48},{80,64},{96,80},{112,96},{128,112},... | collective-permute-start | bytes 884744 | tf_op jit(solution)/shard_map/ppermute | solution.py:38
  18.2 158.1 %collective-permute-start = (f32[6,3,32,128]{3,2,0,1:T(8,128)}, f32[6,3,32,128]{3,2,0,1:T(8,128)}, u32[]{:S(2)}, u32[]{:S(2)}) collective-permute-start(f32[6,3,32,128]{3,2,0,1:T(8,128)} %get-tuple-element.30), channel_id=1, source_target_pairs={{0,16},{16,32},{32,48},{48,64},{64,80},{80,96},{96,112},{112,128},... | collective-permute-start | bytes 884744 | tf_op jit(solution)/shard_map/ppermute | solution.py:37
  79.0 4.8 %copy-start.12 = (s32[25]{0:T(128)S(1)}, s32[25]{0:T(128)}, u32[]{:S(2)}) copy-start(s32[25]{0:T(128)} %param.7) | copy-start | bytes 304
  99.8 102.1 %all-to-all-start = ((f32[16,10,4096]{2,1,0:T(8,128)}), f32[16,10,4096]{2,1,0:T(8,128)}, u32[]{:S(2)}, u32[]{:S(2)}) async-start(f32[16,10,4096]{2,1,0:T(8,128)} %reshape.161), calls=%async_computation | async-start | bytes 8388608 | tf_op jit(solution)/shard_map/all_to_all | solution.py:26
  105.4 3.2 copy-start
  134.5 1.4 copy-start.4
  162.2 13.0 %copy-start.11 = (f32[6,32,128]{2,1,0:T(8,128)S(1)}, f32[6,32,128]{2,1,0:T(8,128)}, u32[]{:S(2)}) copy-start(f32[6,32,128]{2,1,0:T(8,128)} %get-tuple-element.29) | copy-start | bytes 294916
  162.2 14.1 %copy-start.10 = (f32[6,32,128]{2,1,0:T(8,128)S(1)}, f32[6,32,128]{2,1,0:T(8,128)}, u32[]{:S(2)}) copy-start(f32[6,32,128]{2,1,0:T(8,128)} %get-tuple-element.28) | copy-start | bytes 294916
  176.3 0.7 copy-start.7
  177.3 1.4 copy-start.2
  210.6 12.4 %all-to-all-start.1 = ((f32[16,1,2560]{2,1,0:T(1,128)}), f32[16,1,2560]{2,1,0:T(1,128)S(1)}, u32[]{:S(2)}, u32[]{:S(2)}) async-start(f32[16,1,2560]{2,1,0:T(1,128)} %reshape.206), calls=%async_computation.1 | async-start | bytes 327680 | tf_op jit(solution)/shard_map/all_to_all | solution.py:207
  216.6 89.0 %all-gather.2.cloned.1.call-start = ((), (), s32[]{:S(2)}) async-start(), calls=%async_computation.2 | async-start | bytes 2785280 | tf_op jit(solution)/shard_map/all_gather | solution.py:208
  233.5 4.0 %copy-start.3 = (f32[6,22,32,128]{3,2,0,1:T(8,128)S(1)}, f32[6,22,32,128]{3,2,0,1:T(8,128)}, u32[]{:S(2)}) copy-start(f32[6,22,32,128]{3,2,0,1:T(8,128)} %copy-done.2) | copy-start | bytes 6488068
  237.4 2.6 copy-start.8
  237.4 2.6 copy-start.9
  240.0 11.3 %copy-start.5 = (f32[6,16,33,128]{3,2,0,1:T(8,128)S(1)}, f32[6,16,33,128]{3,2,0,1:T(8,128)}, u32[]{:S(2)}) copy-start(f32[6,16,33,128]{3,2,0,1:T(8,128)} %divide_add_fusion.1) | copy-start | bytes 4866052
  240.0 11.3 %copy-start.6 = (f32[6,16,32,129]{3,2,0,1:T(8,128)S(1)}, f32[6,16,32,129]{3,2,0,1:T(8,128)}, u32[]{:S(2)}) copy-start(f32[6,16,32,129]{3,2,0,1:T(8,128)} %divide_add_fusion) | copy-start | bytes 4755460
  305.6 1.7 slice-start
  309.0 3.6 %copy-start.1 = (f32[6,16,32,128]{3,2,1,0:T(8,128)S(1)}, f32[6,16,32,128]{3,2,1,0:T(8,128)}, u32[]{:S(2)}) copy-start(f32[6,16,32,128]{3,2,1,0:T(8,128)} %param.5) | copy-start | bytes 4718596
Sparse Core Ops, SparseCore 0:
  233.6 71.9 all-gather.1
where the time goes:
time: 325 us; the launch traced here: 323 us
  local copies, waits for them, and re-layouts  99.8 us (31%)
  other arithmetic  91.9 us (28%)
  waiting for transfers between devices  78.4 us (24%)
  starting transfers between devices  19.9 us (6%)
  matrix products  19.6 us (6%)
  between operations  13.7 us (4%)
    all_gather x1, waiting for transfers between devices, local(): collected = lax.all_gather(relaid, 'gx', axis=0, tiled=True)  50.4 us
    add x3, other arithmetic, sweep_axis(): face_flux = weno_face(*upwind) + weno_face(*downwind)  44 us
    dot_general x1, local copies, waits for them, and re-layouts, local(): jnp.dot(coeff_rows, span_table, preferred_element_type=jnp.float32)  24.7 us
    unnamed x37, local copies, waits for them, and re-layouts  23 us
    all_to_all x1, waiting for transfers between devices, summed_on_arrival(): tiles = lax.all_to_all(cut_along(x, dim, devices), axis, 0, 0, tiled=True)  22.3 us
    another operation x3, other arithmetic  17.4 us
    dot_general x1, matrix products, local(): jnp.dot(coeff_rows, span_table, preferred_element_type=jnp.float32)  14 us
    unnamed x19, other arithmetic  13 us
  transfers between devices with their start and end apart: 7, of which 3 were waited for; matrix products, arithmetic and copies ran while one was open for 55% of the time, Pallas kernels for 0%

commit v1 on v0

v1 whole, which is shorter than its diff:
```python
import math

import jax, jax.numpy as jnp
from jax import lax
from jax.experimental import pallas as pl
from jax.experimental.pallas import tpu as pltpu
from jax.sharding import PartitionSpec as P
import numpy as np

F32 = jnp.float32
NXL, NZL, NYL = 16, 32, 128


def flux_parts(q, n):
    r, m1, m2, m3, en, ev = q
    rinv = 1.0 / r
    un = q[n] * rinv
    ke = (m1 * m1 + m2 * m2 + m3 * m3) * (0.5 * rinv)
    p = (en - ke - ev) * (1.0 / 2.5)
    s = jnp.abs(un) + jnp.sqrt(1.4 * (p * rinv))
    h = 0.5 * un
    g = [q[c] * h for c in range(6)]
    g[n] = g[n] + 0.5 * p
    g[4] = g[4] + p * h
    return g, 0.5 * s


def ratio(num, den):
    return num * pl.reciprocal(den, approx=False)


def correction(d2, d3, e0, e1, e2):
    d2s = d2 * d2 + 1e-6
    b0 = d2s + e0 * (d2 + (4.0 / 3.0) * e0)
    b1 = d2s + e1 * (d2 + (4.0 / 3.0) * e1)
    b2 = (d3 * d3 + 1e-6) + e2 * ((4.0 / 3.0) * e2 - d3)
    p0, p1, p2 = b0 * b0, b1 * b1, b2 * b2
    w0 = p1 * p2
    w1 = 6.0 * (p0 * p2)
    w2 = 3.0 * (p0 * p1)
    num = e0 * w0 + e1 * w1 + (e1 + 0.5 * (e1 - e2)) * w2
    return ratio(num, w0 + w1 + w2)


def face_value(a, gs, dg, dq, eg, eq):
    ad = [a * x for x in dq]
    ae = [a * x for x in eq]
    pd2, pd3 = dg[0] + ad[0], dg[1] + ad[1]
    md2, md3 = ad[2] - dg[2], ad[1] - dg[1]
    pe = [eg[i] + ae[i] for i in (0, 1, 2)]
    me = [eg[i] - ae[i] for i in (3, 2, 1)]
    lead = (gs - ad[1]) + 0.5 * (pd2 + md2)
    return lead + (1.0 / 3.0) * (correction(pd2, pd3, *pe) + correction(md2, md3, *me))


def face_sweep(qr, gr, ar, tr, comps, n, rows, unroll, tick):
    chunks = rows // 8

    def outer(t, _):
        c = t // chunks
        r0 = (t % chunks) * 8
        at = lambda ref, i: ref[c, pl.ds(pl.multiple_of(i * rows + r0, 8), 8), :]

        def advance(state, f):
            dq, dg, eq, eg = state
            dqn = at(qr, f + 5) - at(qr, f + 4)
            dgn = at(gr, f + 5) - at(gr, f + 4)
            eqn, egn = dqn - dq[2], dgn - dg[2]
            return (dq[0], dq[1], dq[2], dqn), (dg[0], dg[1], dg[2], dgn), (*eq, eqn), (*eg, egn)

        def one(state, f):
            dq, dg, eq, eg = advance(state, f)
            a = ar[pl.ds(pl.multiple_of(f * rows + r0, 8), 8), :]
            gs = at(gr, f + 2) + at(gr, f + 3)
            val = face_value(a, gs, dg[:3], dq[:3], eg, eq)
            return (dq[1:], dg[1:], eq[1:], eg[1:]), val

        qs = [at(qr, i) for i in range(5)]
        gs = [at(gr, i) for i in range(5)]
        dq = [qs[i + 1] - qs[i] for i in range(4)]
        dg = [gs[i + 1] - gs[i] for i in range(4)]
        eq = [dq[i + 1] - dq[i] for i in range(3)]
        eg = [dg[i + 1] - dg[i] for i in range(3)]
        state = (tuple(dq[1:]), tuple(dg[1:]), tuple(eq), tuple(eg))
        state, prev = one(state, 0)

        def inner(b, carry):
            state, prev = carry
            for k in range(unroll):
                f = b * unroll + k + 1
                state, val = one(state, f)
                tr[c, pl.ds(pl.multiple_of((f - 1) * rows + r0, 8), 8), :] = val - prev
                prev = val
            tick(t * (n // unroll) + b)
            return state, prev

        lax.fori_loop(0, n // unroll, inner, (state, prev))
        return 0

    lax.fori_loop(0, comps * chunks, outer, 0)


def speed_sweep(sr, ar, n, rows):
    def body(f, _):
        for r0 in range(0, rows, 8):
            ld = lambda i: sr[pl.ds(pl.multiple_of(i * rows + r0, 8), 8), :]
            m = ld(f)
            for o in range(1, 6):
                m = jnp.maximum(m, ld(f + o))
            ar[pl.ds(pl.multiple_of(f * rows + r0, 8), 8), :] = m
        return 0

    lax.fori_loop(0, n + 1, body, 0)


def flux_sweep(qr, gr, sr, first, count, normal):
    def body(i, _):
        at = pl.ds(pl.multiple_of(i * 8, 8), 8)
        g, s = flux_parts([qr[c, at, :] for c in range(6)], normal)
        for c in range(6):
            gr[c, at, :] = g[c]
        sr[at, :] = s
        return 0

    lax.fori_loop(first, first + count, body, 0, unroll=2)


def transpose_in(qx, tq, qy, gy, sy, tick):
    def block(blk, _):
        for c in range(6):
            x = qx[c, pl.ds(pl.multiple_of(96 + blk * 128, 32), 128), :]
            tq[c] = x.T

        def rows(y, _):
            y0 = pl.multiple_of(y * 8, 8)
            q = [tq[c, pl.ds(y0, 8), :] for c in range(6)]
            g, s = flux_parts(q, 2)
            base = (3 + y0) * 8
            for c in range(6):
                spot = pl.ds(base + (c % 2) * 4 + blk, 8, stride=8)
                qy[c // 2, spot, :] = q[c]
                gy[c // 2, spot, :] = g[c]
            sy[pl.ds(base + blk, 8, stride=8), :] = s
            sy[pl.ds(base + 4 + blk, 8, stride=8), :] = s
            return 0

        lax.fori_loop(0, 16, rows, 0)
        r, m1, m2, m3, en, ev = [tq[c, 0:8, :] for c in range(6)]
        rinv = 1.0 / r
        ke = (m1 * m1 + m2 * m2 + m3 * m3) * (0.5 * rinv)
        temp = (en - ke - ev) * (1.0 / 2.5) * rinv
        ghost = [r, -m1, -m2, -m3, en - 2.5 * r * (temp - 0.36 / temp), ev]
        g, s = flux_parts(ghost, 2)
        for k in range(3):
            for c in range(6):
                spot = pl.ds((2 - k) * 8 + (c % 2) * 4 + blk, 1)
                qy[c // 2, spot, :] = ghost[c][k : k + 1]
                gy[c // 2, spot, :] = g[c][k : k + 1]
            sy[pl.ds((2 - k) * 8 + blk, 1), :] = s[k : k + 1]
            sy[pl.ds((2 - k) * 8 + 4 + blk, 1), :] = s[k : k + 1]
        tick(blk)
        return 0

    lax.fori_loop(0, 4, block, 0)
    for k in range(3):
        src, dst = pl.ds(130 * 8, 8), pl.ds((131 + k) * 8, 8)
        for c in range(3):
            qy[c, dst, :] = qy[c, src, :]
            gy[c, dst, :] = gy[c, src, :]
        sy[dst, :] = sy[src, :]


def swap_in(qx, qz):
    def body(z, _):
        for c in range(6):
            for x0 in (0, 8):
                v = qx[c, pl.ds((3 + x0) * 32 + z, 8, stride=32), :]
                qz[c, pl.ds(pl.multiple_of((3 + z) * 16 + x0, 8), 8), :] = v
        return 0

    lax.fori_loop(0, 32, body, 0)


def combine(qx, tx, tz, ty, out, strength):
    def block(blk, _):
        for c in range(6):
            t = ty[c // 2, pl.ds((c % 2) * 4 + blk, 128, stride=8), :].T
            for k in range(4):
                x = blk * 4 + k
                span = tz[c, pl.ds(x, 32, stride=16), :]
                at = pl.ds(pl.multiple_of(x * 32, 32), 32)
                q = qx[c, pl.ds(pl.multiple_of(96 + x * 32, 32), 32), :]
                rate = tx[c, at, :] + span + t[k * 32 : k * 32 + 32] + strength(x) * q
                out[c, at, :] = q - 0.05 * rate
        return 0

    lax.fori_loop(0, 4, block, 0)

    def relax(i, _):
        at = pl.ds(pl.multiple_of(96 + i * 8, 8), 8)
        r, m1, m2, m3, en, ev = [qx[c, at, :] for c in range(6)]
        rinv = 1.0 / r
        ke = (m1 * m1 + m2 * m2 + m3 * m3) * (0.5 * rinv)
        p = (en - ke - ev) * (1.0 / 2.5)
        temp = p * rinv
        eq = 2.0 / (jnp.exp(2.0 / temp) - 1.0)
        tau = 0.5 * jnp.exp(1.5 * (jnp.exp(jnp.log(temp) * (-1.0 / 3.0)) - 1.0))
        dst = pl.ds(pl.multiple_of(i * 8, 8), 8)
        out[5, dst, :] = out[5, dst, :] + 0.05 * ((r * eq - ev) * p / tau)
        return 0

    lax.fori_loop(0, 64, relax, 0, unroll=2)


def weno_scratch():
    v = lambda *s: pltpu.VMEM(s, F32)
    return dict(
        qx=v(6, 22 * 32, 128), gx=v(6, 22 * 32, 128), sx=v(22 * 32, 128), ax=v(17 * 32, 128), tx=v(6, 16 * 32, 128),
        qz=v(6, 38 * 16, 128), gz=v(6, 38 * 16, 128), sz=v(38 * 16, 128), az=v(33 * 16, 128), tz=v(6, 32 * 16, 128),
        tq=v(6, 128, 128), qy=v(3, 134 * 8, 128), gy=v(3, 134 * 8, 128), sy=v(134 * 8, 128), ay=v(129 * 8, 128), ty=v(3, 128 * 8, 128),
    )


MESH = pl.DeviceIdType.MESH
PLANES = 25
STEP, HOP = 2, 4
PIECES = 48
WIRE_TICKS = PIECES * STEP + 7 * HOP


def spectral_kernel(coeff, table, kron, out, acc):
    step = pl.program_id(0)
    both = jnp.concatenate([coeff[0], coeff[1]], axis=1)
    for half in range(2):
        lanes = slice(half * 256, half * 256 + 256)
        re = jnp.dot(both, table[:, half * 256 : half * 256 + 256], preferred_element_type=F32)
        im = jnp.dot(both, table[:, 512 + half * 256 : 768 + half * 256], preferred_element_type=F32)
        re = re.reshape(16, 6, 8, 256)
        im = im.reshape(16, 6, 8, 256)
        for v in range(6):
            modes = jnp.concatenate([re[:, v].reshape(128, 256), im[:, v].reshape(128, 256)], axis=0)
            part = jnp.dot(kron[0], modes.astype(jnp.bfloat16), preferred_element_type=F32)

            @pl.when(step == 0)
            def _():
                acc[v, :, lanes] = part

            @pl.when(step > 0)
            def _():
                acc[v, :, lanes] = acc[v, :, lanes] + part

    @pl.when(step == pl.num_programs(0) - 1)
    def _():
        lane = lax.broadcasted_iota(jnp.int32, (8, 128), 1)
        low64 = lane < 64
        low32 = lane % 64 < 32

        def tiles(t, _):
            v, g = t // 7, t % 7
            for jb in range(4):
                f = [acc[v, pl.ds(pl.multiple_of(g * 32 + i * 8, 8), 8), jb * 128 : jb * 128 + 128] for i in range(4)]
                n0 = jnp.where(low64, f[0], pltpu.roll(f[2], 64, 1))
                n2 = jnp.where(low64, pltpu.roll(f[0], 64, 1), f[2])
                n1 = jnp.where(low64, f[1], pltpu.roll(f[3], 64, 1))
                n3 = jnp.where(low64, pltpu.roll(f[1], 64, 1), f[3])
                for k, (a, b) in enumerate(((n0, n1), (n2, n3))):
                    out[4 * jb + 2 * k, v, g] = jnp.where(low32, a, pltpu.roll(b, 32, 1))
                    out[4 * jb + 2 * k + 1, v, g] = jnp.where(low32, pltpu.roll(a, 96, 1), b)
            return 0

        lax.fori_loop(0, 42, tiles, 0)


def spectral(coeff, feed_plane):
    n = np.arange(512)
    angle = 2.0 * np.pi / 512.0 * ((n[:, None] * n[None, :]) % 512)
    cz, sz = np.cos(angle), np.sin(angle)
    table = jnp.asarray(np.block([[cz, sz], [-sz, cz]]).astype(np.float32)).astype(jnp.bfloat16)
    shape = (4, 224, 256)
    step, row, col = (lax.broadcasted_iota(jnp.int32, shape, d) for d in range(3))
    feed = jnp.pad(feed_plane, (0, 28 - PLANES))
    feed = jnp.broadcast_to(feed[:, None], (28, 8)).reshape(1, 224, 1)
    mode = lax.axis_index("gx") * 64 + step * 16 + (col % 128) // 8
    ids = (feed * mode + 512 * (col // 128)) % 2048
    wave = jnp.cos(2.0 * math.pi / 2048 * ids.astype(F32))
    kron = jnp.where((row % 8 == col % 8) & (row < 8 * PLANES), wave, 0.0).astype(jnp.bfloat16)
    return pl.pallas_call(
        spectral_kernel,
        grid=(4,),
        out_shape=jax.ShapeDtypeStruct((16, 6, 7, 8, 128), F32),
        in_specs=[
            pl.BlockSpec((2, 768, 512), lambda i: (0, i, 0)),
            pl.BlockSpec((1024, 1024), lambda i: (0, 0)),
            pl.BlockSpec((1, 224, 256), lambda i: (i, 0, 0)),
        ],
        out_specs=pl.BlockSpec((16, 6, 7, 8, 128), lambda i: (0, 0, 0, 0, 0)),
        scratch_shapes=[pltpu.VMEM((6, 224, 512), F32)],
        compiler_params=pltpu.CompilerParams(dimension_semantics=("arbitrary",), vmem_limit_bytes=56 * 2**20),
    )(coeff.reshape(2, 3072, 512), table, kron)


def main_kernel(names, q_hbm, part, out, *scratch):
    s = dict(zip(names, scratch))
    qx, qz, land, feed = s["qx"], s["qz"], s["land"], s["feed"]
    gx, gz = lax.axis_index("gx"), lax.axis_index("gz")
    z, xlo = gx % 8, gx // 8
    z_next = {0: xlo * 8 + (z + 1) % 8, 1: xlo * 8 + (z + 7) % 8}
    is_root = z < 2

    load = pltpu.make_async_copy(q_hbm, qx.at[:, 96:608], s["load_sem"])
    load.start()

    barrier = pltpu.get_barrier_semaphore()

    def greet(a, b):
        pl.semaphore_signal(barrier, inc=1, device_id=(a, b), device_id_type=MESH)

    @pl.when(gx < 15)
    def _():
        greet(gx + 1, gz)

    @pl.when(gx > 0)
    def _():
        greet(gx - 1, gz)

    greet(z_next[0], gz)
    greet(z_next[1], gz)
    greet(gx, (gz + 1) % 16)
    greet(gx, (gz + 15) % 16)

    @pl.when(is_root)
    def _():
        def each(b, _):
            @pl.when((xlo == 1) | (b != gz))
            def _():
                greet(z, b)

            @pl.when(xlo == 0)
            def _():
                greet(8 + z, b)

            return 0

        lax.fori_loop(0, 16, each, 0)

    ends = jnp.where((gx == 0) | (gx == 15), 1, 0)
    roots = jnp.where(is_root, jnp.where(xlo == 0, 31, 16), 0)
    pl.semaphore_wait(barrier, 6 - ends + roots)

    def remote(src, dst, ssem, rsem, a, b):
        return pltpu.make_async_remote_copy(
            src_ref=src, dst_ref=dst, send_sem=ssem, recv_sem=rsem, device_id=(a, b), device_id_type=MESH
        )

    lines = []
    for r in range(2):
        for d in range(2):
            pos = (z - r + 15) % 8 if d == 0 else (r + 7 - z) % 8
            lines.append((r, d, pos))

    def piece(r, d, k):
        c = (gz + 8 * d + k // 6) % 16
        return c, k % 6, (slice(0, 4) if r == 0 else slice(4, 7))

    def tick(n):
        for line, (r, d, pos) in enumerate(lines):
            m = n - pos * HOP
            k = m // STEP

            @pl.when((m >= 0) & (m < PIECES * STEP) & (m % STEP == 0))
            def _():
                c, v, g = piece(r, d, k)
                mine, held = part.at[c, v, g], land.at[c, v, g]
                ssem, rsem = s["send_sem"].at[line], s["recv_sem"].at[line, k]
                onward = lambda src: remote(src, held, ssem, rsem, z_next[d], gz)

                @pl.when(pos == 0)
                def _():
                    onward(mine).start()

                @pl.when(pos > 0)
                def _():
                    onward(held).wait_recv()
                    held[...] = held[...] + mine[...]

                @pl.when((pos > 0) & (pos < 7))
                def _():
                    onward(held).start()

                @pl.when(pos == 7)
                def _():
                    place = feed.at[xlo, v, 0 : (4 if r == 0 else 3), gz]
                    here = (xlo == 0) & (c == gz)

                    @pl.when(here)
                    def _():
                        pltpu.make_async_copy(held, place, s["feed_sem"]).start()

                    @pl.when(jnp.logical_not(here))
                    def _():
                        remote(held, place, ssem, s["feed_sem"], r, c).start()

    halo = []
    for i, (src, dst, a, b, ok_send, ok_recv) in enumerate(
        (
            (qx.at[:, 512:608], qx.at[:, 0:96], jnp.minimum(gx + 1, 15), gz, gx < 15, gx > 0),
            (qx.at[:, 96:192], qx.at[:, 608:704], jnp.maximum(gx - 1, 0), gz, gx > 0, gx < 15),
            (qz.at[:, 512:560], qz.at[:, 0:48], gx, (gz + 1) % 16, None, None),
            (qz.at[:, 48:96], qz.at[:, 560:608], gx, (gz + 15) % 16, None, None),
        )
    ):
        halo.append((remote(src, dst, s["halo_send"].at[i], s["halo_recv"].at[i], a, b), ok_send, ok_recv))

    def on(ok, act):
        if ok is None:
            act()
        else:
            pl.when(ok)(act)

    load.wait()
    for copy, ok, _ in halo[:2]:
        on(ok, copy.start)
    swap_in(qx, qz)
    for copy, ok, _ in halo[2:]:
        on(ok, copy.start)
    transpose_in(qx, s["tq"], s["qy"], s["gy"], s["sy"], lambda blk: tick(blk))
    speed_sweep(s["sy"], s["ay"], 128, 8)
    face_sweep(s["qy"], s["gy"], s["ay"], s["ty"], 3, 128, 8, 8, lambda i: tick(i + 4))
    for copy, _, ok in halo[2:]:
        on(ok, copy.wait_recv)
    flux_sweep(qz, s["gz"], s["sz"], 0, 76, 3)
    speed_sweep(s["sz"], s["az"], 32, 16)
    face_sweep(qz, s["gz"], s["az"], s["tz"], 6, 32, 16, 8, lambda i: tick(i + 52))
    for copy, _, ok in halo[:2]:
        on(ok, copy.wait_recv)

    @pl.when(gx == 0)
    def _():
        for i in range(3):
            qx[:, i * 32 : i * 32 + 32] = qx[:, 96:128]

    @pl.when(gx == 15)
    def _():
        for i in range(3):
            qx[:, 608 + i * 32 : 640 + i * 32] = qx[:, 576:608]

    flux_sweep(qx, s["gx"], s["sx"], 0, 88, 1)
    speed_sweep(s["sx"], s["ax"], 16, 32)
    face_sweep(qx, s["gx"], s["ax"], s["tx"], 6, 16, 32, 16, lambda i: tick(i + 100))

    def strength(x):
        plane = gx * 16 + x
        level = 1.0 - plane.astype(F32) * (1.0 / PLANES)
        return jnp.where(plane < PLANES, 2.0 * level * level, 0.0)

    combine(qx, s["tx"], s["tz"], s["ty"], out, strength)

    def drain(n, _):
        tick(n)
        return 0

    lax.fori_loop(124, WIRE_TICKS, drain, 0)

    for r in range(2):

        @pl.when(gx == r)
        def _():
            groups = 4 if r == 0 else 3
            whole = feed.at[:, :, 0:groups]
            pltpu.make_async_copy(whole, whole, s["feed_sem"]).wait()

            def add(v, _):
                for g in range(groups):
                    t = (feed[0, v, g].reshape(128, 128) + feed[1, v, g].reshape(128, 128)).T
                    for i in range(4):
                        x = g * 4 + i
                        at = slice(x * 32, x * 32 + 32)
                        out[v, at, :] = out[v, at, :] + (0.05 * strength(jnp.int32(x))) * t[i * 32 : i * 32 + 32]
                return 0

            lax.fori_loop(0, 6, add, 0)

    for copy, ok, _ in halo:
        on(ok, copy.wait_send)
    for line, (r, d, pos) in enumerate(lines):
        groups = slice(0, 4) if r == 0 else slice(4, 7)
        short = (pos == 7) & (xlo == 0) if d == 0 else None

        def sent(blocks):
            span = land.at[0:blocks, :, groups]
            pltpu.make_async_copy(span, span, s["send_sem"].at[line]).wait()

        if short is None:
            sent(8)
        else:
            pl.when(short)(lambda: sent(7))
            pl.when(jnp.logical_not(short))(lambda: sent(8))


def local(conserved_fields, coeff, feed_plane):
    part = spectral(coeff, feed_plane)
    scratch = weno_scratch()
    scratch.update(
        land=pltpu.VMEM((16, 6, 7, 8, 128), F32),
        feed=pltpu.VMEM((2, 6, 4, 16, 8, 128), F32),
        load_sem=pltpu.SemaphoreType.DMA,
        halo_send=pltpu.SemaphoreType.DMA((4,)),
        halo_recv=pltpu.SemaphoreType.DMA((4,)),
        send_sem=pltpu.SemaphoreType.DMA((4,)),
        recv_sem=pltpu.SemaphoreType.DMA((4, PIECES)),
        feed_sem=pltpu.SemaphoreType.DMA,
    )
    names = list(scratch)
    out = pl.pallas_call(
        lambda *refs: main_kernel(names, *refs),
        out_shape=jax.ShapeDtypeStruct((6, 512, 128), F32),
        in_specs=[pl.BlockSpec(memory_space=pl.ANY), pl.BlockSpec(memory_space=pltpu.VMEM)],
        out_specs=pl.BlockSpec(memory_space=pltpu.VMEM),
        scratch_shapes=list(scratch.values()),
        compiler_params=pltpu.CompilerParams(collective_id=0, has_side_effects=True, vmem_limit_bytes=56 * 2**20),
        name="section",
    )(conserved_fields.reshape(6, 512, 128), part)
    return out.reshape(6, 16, 32, 128)


def solution(mesh):
    placed = (P(None, "gx", "gz", None), P(None, "gx", None, "gz", None), P())
    return jax.shard_map(
        local, mesh=mesh, in_specs=placed, out_specs=P(None, "gx", "gz", None), check_vma=False
    )
```

time: 325 us -> 155 us (0.48)
  the two profiles are of different devices: /device:TPU:8 before, /device:TPU:1 now
where the time goes in v1:
time: 155 us
  Pallas kernels  147 us (95%)
  other arithmetic  4.59 us (3%)
  local copies, waits for them, and re-layouts  3.58 us (2%)
    pallas_call x1, Pallas kernels, local(): pl.pallas_call(lambda *refs: main_kernel(names, *refs), out_shape=jax.Sha...  118 us
    pallas_call x1, Pallas kernels, spectral(): pl.pallas_call(spectral_kernel, grid=(4,), out_shape=jax.ShapeDtypeStruct...  28.8 us
    convert_element_type x1, other arithmetic, spectral(): jnp.where((row % 8 == col % 8) & (row < 8 * PLANES), wave, 0.0)  4.55 us

profile of v1, /device:TPU:1, one launch (start us, length us, event | category | flops | bytes accessed | tf_op | source)
XLA Modules:
  0.0 155.0 jit_solution(12255394276614071194)
XLA Ops:
  0.0 0.7 pad.4
  0.7 0.1 broadcast_in_dim.10
  0.8 0.1 mul.32
  0.9 4.6 %fusion.9.kron = bf16[4,224,256]{2,1,0:T(8,128)(2,1)} fusion(s32[256]{0:T(256)S(1)} %get-tuple-element.9, s32[256]{0:T(256)S(1)} %get-tuple-element.16, s32[256]{0:T(256)S(1)} %get-tuple-element.10, s32[256]{0:T(256)S(1)} %get-tuple-element.14, s32[4]{0:T(128)S(1)} %multiply_add_fusion, s32[224]{0:T(256)S(1)} %mul.32, s32[256]{0:T(256)S(1)} %get-tuple-element.13, ...), kind=kLoop, calls=%fused_computation.19 | loop fusion | flops 9175040 | bytes 468816 | tf_op jit(solution)/shard_map/convert_element_type | solution.py:286
  5.4 28.8 %shard_map.46.refs_1_ = f32[16,6,7,8,128]{4,3,2,1,0:T(8,128)} custom-call(bf16[2,3072,512]{2,1,0:T(8,128)(2,1)} %bitcast.3, bf16[1024,1024]{1,0:T(8,128)(2,1)} %constant.92.table, bf16[4,224,256]{2,1,0:T(8,128)(2,1)} %fusion.9.kron), custom_call_target="tpu_custom_call" | custom-call | tf_op jit(solution)/shard_map/pallas_call | solution.py:287
  34.2 118.0 %section.1 = f32[6,512,128]{2,1,0:T(8,128)} custom-call(f32[6,512,128]{2,1,0:T(8,128)} %bitcast.5, f32[16,6,7,8,128]{4,3,2,1,0:T(8,128)} %shard_map.46.refs_1_), custom_call_target="tpu_custom_call" | custom-call | tf_op jit(solution)/shard_map/section/pallas_call | solution.py:514
  152.2 2.8 %copy.6 = f32[6,16,32,128]{3,2,1,0:T(8,128)} copy(f32[6,16,32,128]{3,2,1,0:T(8,128)} %bitcast.4) | data formatting | bytes 3145728
  (8 shorter events, 0.0 us)

commit v2 on v1

--- a/solution.py
+++ b/solution.py
@@ -223,13 +223,27 @@
 
 MESH = pl.DeviceIdType.MESH
 PLANES = 25
-STEP, HOP = 2, 4
-PIECES = 48
-WIRE_TICKS = PIECES * STEP + 7 * HOP
-
-
-def spectral_kernel(coeff, table, kron, out, acc):
+STEP = 2
+HOP = 9
+PIECES = 24
+AHEAD = 2
+WIRE_TICKS = PIECES * STEP + 8 * HOP
+
+
+def spectral_kernel(coeff, table, wave, out, acc):
     step = pl.program_id(0)
+
+    @pl.when(step == 0)
+    def _():
+        acc[...] = jnp.zeros_like(acc)
+
+    iota = lambda shape, d: lax.broadcasted_iota(jnp.int32, shape, d)
+    rows = jnp.where(iota((224, 32), 0) // 8 == iota((224, 32), 1), 1.0, 0.0).astype(jnp.bfloat16)
+    col = iota((32, 256), 1)
+    cols = jnp.where(col // 128 * 16 + col % 128 // 8 == iota((32, 256), 0), 1.0, 0.0).astype(jnp.bfloat16)
+    wide = jnp.dot(wave[0], cols, preferred_element_type=F32).astype(jnp.bfloat16)
+    wide = jnp.dot(rows, wide, preferred_element_type=F32)
+    kron = jnp.where(iota((224, 256), 0) % 8 == iota((224, 256), 1) % 8, wide, 0.0).astype(jnp.bfloat16)
     both = jnp.concatenate([coeff[0], coeff[1]], axis=1)
     for half in range(2):
         lanes = slice(half * 256, half * 256 + 256)
@@ -239,15 +253,7 @@
         im = im.reshape(16, 6, 8, 256)
         for v in range(6):
             modes = jnp.concatenate([re[:, v].reshape(128, 256), im[:, v].reshape(128, 256)], axis=0)
-            part = jnp.dot(kron[0], modes.astype(jnp.bfloat16), preferred_element_type=F32)
-
-            @pl.when(step == 0)
-            def _():
-                acc[v, :, lanes] = part
-
-            @pl.when(step > 0)
-            def _():
-                acc[v, :, lanes] = acc[v, :, lanes] + part
+            acc[v, :, lanes] += jnp.dot(kron, modes.astype(jnp.bfloat16), preferred_element_type=F32)
 
     @pl.when(step == pl.num_programs(0) - 1)
     def _():
@@ -257,6 +263,7 @@
 
         def tiles(t, _):
             v, g = t // 7, t % 7
+            gz = lax.axis_index("gz")
             for jb in range(4):
                 f = [acc[v, pl.ds(pl.multiple_of(g * 32 + i * 8, 8), 8), jb * 128 : jb * 128 + 128] for i in range(4)]
                 n0 = jnp.where(low64, f[0], pltpu.roll(f[2], 64, 1))
@@ -264,11 +271,11 @@
                 n1 = jnp.where(low64, f[1], pltpu.roll(f[3], 64, 1))
                 n3 = jnp.where(low64, pltpu.roll(f[1], 64, 1), f[3])
                 for k, (a, b) in enumerate(((n0, n1), (n2, n3))):
-                    out[4 * jb + 2 * k, v, g] = jnp.where(low32, a, pltpu.roll(b, 32, 1))
-                    out[4 * jb + 2 * k + 1, v, g] = jnp.where(low32, pltpu.roll(a, 96, 1), b)
+                    out[v, (4 * jb + 2 * k + 16 - gz) % 16, g] = jnp.where(low32, a, pltpu.roll(b, 32, 1))
+                    out[v, (4 * jb + 2 * k + 17 - gz) % 16, g] = jnp.where(low32, pltpu.roll(a, 96, 1), b)
             return 0
 
-        lax.fori_loop(0, 42, tiles, 0)
+        lax.fori_loop(0, 42, tiles, 0, unroll=6)
 
 
 def spectral(coeff, feed_plane):
@@ -276,32 +283,31 @@
     angle = 2.0 * np.pi / 512.0 * ((n[:, None] * n[None, :]) % 512)
     cz, sz = np.cos(angle), np.sin(angle)
     table = jnp.asarray(np.block([[cz, sz], [-sz, cz]]).astype(np.float32)).astype(jnp.bfloat16)
-    shape = (4, 224, 256)
-    step, row, col = (lax.broadcasted_iota(jnp.int32, shape, d) for d in range(3))
-    feed = jnp.pad(feed_plane, (0, 28 - PLANES))
-    feed = jnp.broadcast_to(feed[:, None], (28, 8)).reshape(1, 224, 1)
-    mode = lax.axis_index("gx") * 64 + step * 16 + (col % 128) // 8
-    ids = (feed * mode + 512 * (col // 128)) % 2048
+    shape = (4, 32, 32)
+    step, plane, col = (lax.broadcasted_iota(jnp.int32, shape, d) for d in range(3))
+    feed = jnp.pad(feed_plane, (0, 32 - PLANES)).reshape(1, 32, 1)
+    mode = lax.axis_index("gx") * 64 + step * 16 + col % 16
+    ids = (feed * mode + 512 * (col // 16)) % 2048
     wave = jnp.cos(2.0 * math.pi / 2048 * ids.astype(F32))
-    kron = jnp.where((row % 8 == col % 8) & (row < 8 * PLANES), wave, 0.0).astype(jnp.bfloat16)
+    wave = jnp.where(plane < PLANES, wave, 0.0).astype(jnp.bfloat16)
     return pl.pallas_call(
         spectral_kernel,
         grid=(4,),
-        out_shape=jax.ShapeDtypeStruct((16, 6, 7, 8, 128), F32),
+        out_shape=jax.ShapeDtypeStruct((6, 16, 7, 8, 128), F32),
         in_specs=[
             pl.BlockSpec((2, 768, 512), lambda i: (0, i, 0)),
             pl.BlockSpec((1024, 1024), lambda i: (0, 0)),
-            pl.BlockSpec((1, 224, 256), lambda i: (i, 0, 0)),
+            pl.BlockSpec((1, 32, 32), lambda i: (i, 0, 0)),
         ],
-        out_specs=pl.BlockSpec((16, 6, 7, 8, 128), lambda i: (0, 0, 0, 0, 0)),
+        out_specs=pl.BlockSpec((6, 16, 7, 8, 128), lambda i: (0, 0, 0, 0, 0)),
         scratch_shapes=[pltpu.VMEM((6, 224, 512), F32)],
         compiler_params=pltpu.CompilerParams(dimension_semantics=("arbitrary",), vmem_limit_bytes=56 * 2**20),
-    )(coeff.reshape(2, 3072, 512), table, kron)
+    )(coeff.reshape(2, 3072, 512), table, wave)
 
 
 def main_kernel(names, q_hbm, part, out, *scratch):
     s = dict(zip(names, scratch))
-    qx, qz, land, feed = s["qx"], s["qz"], s["land"], s["feed"]
+    qx, qz, land, swap, feed = s["qx"], s["qz"], s["land"], s["swap"], s["feed"]
     gx, gz = lax.axis_index("gx"), lax.axis_index("gz")
     z, xlo = gx % 8, gx // 8
     z_next = {0: xlo * 8 + (z + 1) % 8, 1: xlo * 8 + (z + 7) % 8}
@@ -323,6 +329,7 @@
     def _():
         greet(gx - 1, gz)
 
+    greet((gx + 8) % 16, gz)
     greet(z_next[0], gz)
     greet(z_next[1], gz)
     greet(gx, (gz + 1) % 16)
@@ -345,60 +352,93 @@
 
     ends = jnp.where((gx == 0) | (gx == 15), 1, 0)
     roots = jnp.where(is_root, jnp.where(xlo == 0, 31, 16), 0)
-    pl.semaphore_wait(barrier, 6 - ends + roots)
+    pl.semaphore_wait(barrier, 7 - ends + roots)
 
     def remote(src, dst, ssem, rsem, a, b):
         return pltpu.make_async_remote_copy(
             src_ref=src, dst_ref=dst, send_sem=ssem, recv_sem=rsem, device_id=(a, b), device_id_type=MESH
         )
 
-    lines = []
-    for r in range(2):
-        for d in range(2):
-            pos = (z - r + 15) % 8 if d == 0 else (r + 7 - z) % 8
-            lines.append((r, d, pos))
-
-    def piece(r, d, k):
-        c = (gz + 8 * d + k // 6) % 16
-        return c, k % 6, (slice(0, 4) if r == 0 else slice(4, 7))
+    groups = (slice(0, 4), slice(4, 7))
+    every = slice(0, 7)
+    lines = ((0, (z + 7) % 8), (1, (8 - z) % 8))
+
+    def exchange(d, i):
+        block = (i // 2, pl.ds(8 * d + i % 2 * 4, 4))
+        return remote(part.at[1 - xlo, *block], swap.at[block], s["swap_send"], s["swap_recv"].at[d, i], (gx + 8) % 16, gz)
 
     def tick(n):
-        for line, (r, d, pos) in enumerate(lines):
-            m = n - pos * HOP
-            k = m // STEP
-
-            @pl.when((m >= 0) & (m < PIECES * STEP) & (m % STEP == 0))
-            def _():
-                c, v, g = piece(r, d, k)
-                mine, held = part.at[c, v, g], land.at[c, v, g]
-                ssem, rsem = s["send_sem"].at[line], s["recv_sem"].at[line, k]
-                onward = lambda src: remote(src, held, ssem, rsem, z_next[d], gz)
+        for d, pos in lines:
+            first, second = groups[d], groups[1 - d]
+
+            def turn(k, last):
+                v, e = k // 8, 8 * d + k % 8
+                held = lambda g: land.at[v, e, g]
+                mine = lambda g: part[xlo, v, e, g] + swap[v, e, g]
+                ssem, rsem = s["send_sem"].at[d], s["recv_sem"].at[d, k]
+                onward = lambda g: remote(held(g), held(g), ssem, rsem, z_next[d], gz)
+
+                def add(g):
+                    held(g)[...] = held(g)[...] + mine(g)
+
+                def deliver(r):
+                    c = (gz + e) % 16
+                    place = feed.at[3 * xlo + v, gz, 0 : 4 - r]
+                    here = (xlo == 0) & (c == gz)
+
+                    @pl.when(here)
+                    def _():
+                        pltpu.make_async_copy(held(groups[r]), place, s["feed_sem"]).start()
+
+                    @pl.when(jnp.logical_not(here))
+                    def _():
+                        remote(held(groups[r]), place, ssem, s["feed_sem"], r, c).start()
+
+                if last:
+                    onward(second).wait_recv()
+                    add(second)
+                    deliver(1 - d)
+                    return
+
+                @pl.when(k % 4 == 0)
+                def _():
+                    exchange(d, k // 4).wait_recv()
+
+                    @pl.when(k < PIECES - 4 * AHEAD)
+                    def _():
+                        exchange(d, k // 4 + AHEAD).start()
 
                 @pl.when(pos == 0)
                 def _():
-                    onward(mine).start()
-
-                @pl.when(pos > 0)
+                    held(first)[...] = mine(first)
+                    onward(first).start()
+
+                @pl.when(pos == 1)
                 def _():
-                    onward(held).wait_recv()
-                    held[...] = held[...] + mine[...]
-
-                @pl.when((pos > 0) & (pos < 7))
+                    held(second)[...] = mine(second)
+                    onward(first).wait_recv()
+                    add(first)
+                    onward(every).start()
+
+                @pl.when((pos > 1) & (pos < 7))
                 def _():
-                    onward(held).start()
+                    onward(every).wait_recv()
+                    add(every)
+                    onward(every).start()
 
                 @pl.when(pos == 7)
                 def _():
-                    place = feed.at[xlo, v, 0 : (4 if r == 0 else 3), gz]
-                    here = (xlo == 0) & (c == gz)
-
-                    @pl.when(here)
-                    def _():
-                        pltpu.make_async_copy(held, place, s["feed_sem"]).start()
-
-                    @pl.when(jnp.logical_not(here))
-                    def _():
-                        remote(held, place, ssem, s["feed_sem"], r, c).start()
+                    onward(every).wait_recv()
+                    add(every)
+                    onward(second).start()
+                    deliver(d)
+
+            def due(place, ok, last):
+                m = n - place * HOP
+                pl.when(ok & (m >= 0) & (m < PIECES * STEP) & (m % STEP == 0))(lambda: turn(m // STEP, last))
+
+            due(pos, pos >= 0, False)
+            due(8, pos == 0, True)
 
     halo = []
     for i, (src, dst, a, b, ok_send, ok_recv) in enumerate(
@@ -417,6 +457,12 @@
         else:
             pl.when(ok)(act)
 
+    def exchanges(i, _):
+        exchange(0, i).start()
+        exchange(1, i).start()
+        return 0
+
+    lax.fori_loop(0, AHEAD, exchanges, 0)
     load.wait()
     for copy, ok, _ in halo[:2]:
         on(ok, copy.start)
@@ -465,13 +511,13 @@
 
         @pl.when(gx == r)
         def _():
-            groups = 4 if r == 0 else 3
-            whole = feed.at[:, :, 0:groups]
+            count = 4 if r == 0 else 3
+            whole = feed.at[:, :, 0:count]
             pltpu.make_async_copy(whole, whole, s["feed_sem"]).wait()
 
             def add(v, _):
-                for g in range(groups):
-                    t = (feed[0, v, g].reshape(128, 128) + feed[1, v, g].reshape(128, 128)).T
+                for g in range(count):
+                    t = feed[v, :, g].reshape(128, 128).T
                     for i in range(4):
                         x = g * 4 + i
                         at = slice(x * 32, x * 32 + 32)
@@ -482,32 +528,37 @@
 
     for copy, ok, _ in halo:
         on(ok, copy.wait_send)
-    for line, (r, d, pos) in enumerate(lines):
-        groups = slice(0, 4) if r == 0 else slice(4, 7)
-        short = (pos == 7) & (xlo == 0) if d == 0 else None
-
-        def sent(blocks):
-            span = land.at[0:blocks, :, groups]
-            pltpu.make_async_copy(span, span, s["send_sem"].at[line]).wait()
-
-        if short is None:
-            sent(8)
+    pltpu.make_async_copy(swap, swap, s["swap_send"]).wait()
+    for d, pos in lines:
+
+        def sent(blocks, g):
+            span = land.at[:, blocks, g]
+            pltpu.make_async_copy(span, span, s["send_sem"].at[d]).wait()
+
+        if d == 1:
+            sent(slice(0, 8), every)
         else:
-            pl.when(short)(lambda: sent(7))
-            pl.when(jnp.logical_not(short))(lambda: sent(8))
+            sent(slice(0, 7), every)
+            own = xlo == 0
+            pl.when(own & (pos == 0))(lambda: sent(slice(7, 8), groups[0]))
+            pl.when(own & (pos == 7))(lambda: sent(slice(7, 8), groups[1]))
+            pl.when(jnp.logical_not(own) | ((pos > 0) & (pos < 7)))(lambda: sent(slice(7, 8), every))
 
 
 def local(conserved_fields, coeff, feed_plane):
     part = spectral(coeff, feed_plane)
     scratch = weno_scratch()
     scratch.update(
-        land=pltpu.VMEM((16, 6, 7, 8, 128), F32),
-        feed=pltpu.VMEM((2, 6, 4, 16, 8, 128), F32),
+        land=pltpu.VMEM((3, 16, 7, 8, 128), F32),
+        swap=pltpu.VMEM((3, 16, 7, 8, 128), F32),
+        feed=pltpu.VMEM((6, 16, 4, 8, 128), F32),
         load_sem=pltpu.SemaphoreType.DMA,
         halo_send=pltpu.SemaphoreType.DMA((4,)),
         halo_recv=pltpu.SemaphoreType.DMA((4,)),
-        send_sem=pltpu.SemaphoreType.DMA((4,)),
-        recv_sem=pltpu.SemaphoreType.DMA((4, PIECES)),
+        send_sem=pltpu.SemaphoreType.DMA((2,)),
+        recv_sem=pltpu.SemaphoreType.DMA((2, PIECES)),
+        swap_send=pltpu.SemaphoreType.DMA,
+        swap_recv=pltpu.SemaphoreType.DMA((2, 6)),
         feed_sem=pltpu.SemaphoreType.DMA,
     )
     names = list(scratch)
@@ -519,7 +570,7 @@
         scratch_shapes=list(scratch.values()),
         compiler_params=pltpu.CompilerParams(collective_id=0, has_side_effects=True, vmem_limit_bytes=56 * 2**20),
         name="section",
-    )(conserved_fields.reshape(6, 512, 128), part)
+    )(conserved_fields.reshape(6, 512, 128), part.reshape(2, 3, 16, 7, 8, 128))
     return out.reshape(6, 16, 32, 128)
 
 

time: 155 us -> 100 us (0.65)
  Pallas kernels: 147 us -> 95.1 us
  other arithmetic: 4.59 us -> 0.98 us
    pallas_call x1, Pallas kernels: 118 us -> 77 us  [local(): pl.pallas_call(lambda *refs: main_kernel(names, *refs), out_shape=jax.Sha...]
    pallas_call x1, Pallas kernels: 28.8 us -> 18.2 us  [spectral(): pl.pallas_call(spectral_kernel, grid=(4,), out_shape=jax.ShapeDtypeStruct...]
    convert_element_type x1, other arithmetic: 4.55 us -> 0.95 us  [spectral(): wave = jnp.where(plane < PLANES, wave, 0.0).astype(jnp.bfloat16)]
where the time goes in v2:
time: 100 us; the launch traced here: 99.6 us
  Pallas kernels  95.1 us (95%)
  local copies, waits for them, and re-layouts  3.42 us (3%)
    pallas_call x1, Pallas kernels, local(): pl.pallas_call(lambda *refs: main_kernel(names, *refs), out_shape=jax.Sha...  77 us
    pallas_call x1, Pallas kernels, spectral(): pl.pallas_call(spectral_kernel, grid=(4,), out_shape=jax.ShapeDtypeStruct...  18.2 us
    unnamed x1, local copies, waits for them, and re-layouts  2.76 us

profile of v2, /device:TPU:1, one launch (start us, length us, event | category | flops | bytes accessed | tf_op | source)
XLA Modules:
  0.0 99.6 jit_solution(13544897851129578254)
XLA Ops:
  0.0 0.7 pad.4
  0.7 1.0 fusion.5.wave
  1.7 18.2 %shard_map.46 = f32[6,16,7,8,128]{4,3,2,1,0:T(8,128)} custom-call(bf16[2,3072,512]{2,1,0:T(8,128)(2,1)} %bitcast.6, bf16[1024,1024]{1,0:T(8,128)(2,1)} %constant.65.table, bf16[4,32,32]{2,1,0:T(8,128)(2,1)} %fusion.5.wave), custom_call_target="tpu_custom_call" | custom-call | tf_op jit(solution)/shard_map/pallas_call | solution.py:293
  19.8 77.0 %section.1 = f32[6,512,128]{2,1,0:T(8,128)} custom-call(f32[6,512,128]{2,1,0:T(8,128)} %bitcast.7, f32[2,3,16,7,8,128]{5,4,3,2,1,0:T(8,128)} %bitcast.4), custom_call_target="tpu_custom_call" | custom-call | tf_op jit(solution)/shard_map/section/pallas_call | solution.py:565
  96.8 2.8 %copy.6 = f32[6,16,32,128]{3,2,1,0:T(8,128)} copy(f32[6,16,32,128]{3,2,1,0:T(8,128)} %bitcast.5) | data formatting | bytes 3145728
  (5 shorter events, 0.0 us)

commit v3 on v2

--- a/solution.py
+++ b/solution.py
@@ -224,89 +224,63 @@
 MESH = pl.DeviceIdType.MESH
 PLANES = 25
 STEP = 2
-HOP = 9
+HOP = 11
 PIECES = 24
-AHEAD = 2
 WIRE_TICKS = PIECES * STEP + 8 * HOP
 
 
-def spectral_kernel(coeff, table, wave, out, acc):
-    step = pl.program_id(0)
-
-    @pl.when(step == 0)
-    def _():
-        acc[...] = jnp.zeros_like(acc)
-
+def kron_table(wave, kron):
     iota = lambda shape, d: lax.broadcasted_iota(jnp.int32, shape, d)
     rows = jnp.where(iota((224, 32), 0) // 8 == iota((224, 32), 1), 1.0, 0.0).astype(jnp.bfloat16)
-    col = iota((32, 256), 1)
-    cols = jnp.where(col // 128 * 16 + col % 128 // 8 == iota((32, 256), 0), 1.0, 0.0).astype(jnp.bfloat16)
-    wide = jnp.dot(wave[0], cols, preferred_element_type=F32).astype(jnp.bfloat16)
+    col = iota((128, 1024), 1)
+    cols = jnp.where(col // 512 * 64 + col % 512 // 8 == iota((128, 1024), 0), 1.0, 0.0).astype(jnp.bfloat16)
+    wide = jnp.dot(wave[...], cols, preferred_element_type=F32).astype(jnp.bfloat16)
     wide = jnp.dot(rows, wide, preferred_element_type=F32)
-    kron = jnp.where(iota((224, 256), 0) % 8 == iota((224, 256), 1) % 8, wide, 0.0).astype(jnp.bfloat16)
-    both = jnp.concatenate([coeff[0], coeff[1]], axis=1)
-    for half in range(2):
-        lanes = slice(half * 256, half * 256 + 256)
-        re = jnp.dot(both, table[:, half * 256 : half * 256 + 256], preferred_element_type=F32)
-        im = jnp.dot(both, table[:, 512 + half * 256 : 768 + half * 256], preferred_element_type=F32)
-        re = re.reshape(16, 6, 8, 256)
-        im = im.reshape(16, 6, 8, 256)
-        for v in range(6):
-            modes = jnp.concatenate([re[:, v].reshape(128, 256), im[:, v].reshape(128, 256)], axis=0)
-            acc[v, :, lanes] += jnp.dot(kron, modes.astype(jnp.bfloat16), preferred_element_type=F32)
-
-    @pl.when(step == pl.num_programs(0) - 1)
-    def _():
-        lane = lax.broadcasted_iota(jnp.int32, (8, 128), 1)
-        low64 = lane < 64
-        low32 = lane % 64 < 32
-
-        def tiles(t, _):
-            v, g = t // 7, t % 7
-            gz = lax.axis_index("gz")
-            for jb in range(4):
-                f = [acc[v, pl.ds(pl.multiple_of(g * 32 + i * 8, 8), 8), jb * 128 : jb * 128 + 128] for i in range(4)]
-                n0 = jnp.where(low64, f[0], pltpu.roll(f[2], 64, 1))
-                n2 = jnp.where(low64, pltpu.roll(f[0], 64, 1), f[2])
-                n1 = jnp.where(low64, f[1], pltpu.roll(f[3], 64, 1))
-                n3 = jnp.where(low64, pltpu.roll(f[1], 64, 1), f[3])
-                for k, (a, b) in enumerate(((n0, n1), (n2, n3))):
-                    out[v, (4 * jb + 2 * k + 16 - gz) % 16, g] = jnp.where(low32, a, pltpu.roll(b, 32, 1))
-                    out[v, (4 * jb + 2 * k + 17 - gz) % 16, g] = jnp.where(low32, pltpu.roll(a, 96, 1), b)
-            return 0
-
-        lax.fori_loop(0, 42, tiles, 0, unroll=6)
-
-
-def spectral(coeff, feed_plane):
+    kron[...] = jnp.where(iota((224, 1024), 0) % 8 == iota((224, 1024), 1) % 8, wide, 0.0).astype(jnp.bfloat16)
+
+
+def spectral(i, raw, rows, table, kron, modes, sums, put, tick):
+    for p in range(2):
+        rows[:, p * 512 : p * 512 + 512] = raw[i % 2, p].reshape(512, 512)
+    for h in range(2):
+        for p in range(2):
+            at = p * 512 + h * 256
+            span = jnp.dot(rows[...], table[:, at : at + 256], preferred_element_type=F32)
+            modes[p * 512 : p * 512 + 512, :] = span.astype(jnp.bfloat16)
+            tick(h * 3 + p)
+        sums[:, h * 256 : h * 256 + 256] = jnp.dot(kron[...], modes[...], preferred_element_type=F32)
+        tick(h * 3 + 2)
+    lane = lax.broadcasted_iota(jnp.int32, (8, 128), 1)
+    low64 = lane < 64
+    low32 = lane % 64 < 32
+    for g in range(7):
+        for jb in range(4):
+            f = [sums[g * 32 + n * 8 : g * 32 + n * 8 + 8, jb * 128 : jb * 128 + 128] for n in range(4)]
+            n0 = jnp.where(low64, f[0], pltpu.roll(f[2], 64, 1))
+            n2 = jnp.where(low64, pltpu.roll(f[0], 64, 1), f[2])
+            n1 = jnp.where(low64, f[1], pltpu.roll(f[3], 64, 1))
+            n3 = jnp.where(low64, pltpu.roll(f[1], 64, 1), f[3])
+            for k, (a, b) in enumerate(((n0, n1), (n2, n3))):
+                put(4 * jb + 2 * k, g, jnp.where(low32, a, pltpu.roll(b, 32, 1)))
+                put(4 * jb + 2 * k + 1, g, jnp.where(low32, pltpu.roll(a, 96, 1), b))
+
+
+def tables(feed_plane):
     n = np.arange(512)
     angle = 2.0 * np.pi / 512.0 * ((n[:, None] * n[None, :]) % 512)
     cz, sz = np.cos(angle), np.sin(angle)
     table = jnp.asarray(np.block([[cz, sz], [-sz, cz]]).astype(np.float32)).astype(jnp.bfloat16)
-    shape = (4, 32, 32)
-    step, plane, col = (lax.broadcasted_iota(jnp.int32, shape, d) for d in range(3))
-    feed = jnp.pad(feed_plane, (0, 32 - PLANES)).reshape(1, 32, 1)
-    mode = lax.axis_index("gx") * 64 + step * 16 + col % 16
-    ids = (feed * mode + 512 * (col // 16)) % 2048
+    plane, col = (lax.broadcasted_iota(jnp.int32, (32, 128), d) for d in range(2))
+    feed = jnp.pad(feed_plane, (0, 32 - PLANES)).reshape(32, 1)
+    mode = lax.axis_index("gx") * 64 + col % 64
+    ids = (feed * mode + 512 * (col // 64)) % 2048
     wave = jnp.cos(2.0 * math.pi / 2048 * ids.astype(F32))
-    wave = jnp.where(plane < PLANES, wave, 0.0).astype(jnp.bfloat16)
-    return pl.pallas_call(
-        spectral_kernel,
-        grid=(4,),
-        out_shape=jax.ShapeDtypeStruct((6, 16, 7, 8, 128), F32),
-        in_specs=[
-            pl.BlockSpec((2, 768, 512), lambda i: (0, i, 0)),
-            pl.BlockSpec((1024, 1024), lambda i: (0, 0)),
-            pl.BlockSpec((1, 32, 32), lambda i: (i, 0, 0)),
-        ],
-        out_specs=pl.BlockSpec((6, 16, 7, 8, 128), lambda i: (0, 0, 0, 0, 0)),
-        scratch_shapes=[pltpu.VMEM((6, 224, 512), F32)],
-        compiler_params=pltpu.CompilerParams(dimension_semantics=("arbitrary",), vmem_limit_bytes=56 * 2**20),
-    )(coeff.reshape(2, 3072, 512), table, wave)
-
-
-def main_kernel(names, q_hbm, part, out, *scratch):
+    return table, jnp.where(plane < PLANES, wave, 0.0).astype(jnp.bfloat16)
+
+
+def main_kernel(names, q_hbm, coeff, table, wave, out, *scratch):
     s = dict(zip(names, scratch))
+    part = s["part"]
     qx, qz, land, swap, feed = s["qx"], s["qz"], s["land"], s["swap"], s["feed"]
     gx, gz = lax.axis_index("gx"), lax.axis_index("gz")
     z, xlo = gx % 8, gx // 8
@@ -315,6 +289,14 @@
 
     load = pltpu.make_async_copy(q_hbm, qx.at[:, 96:608], s["load_sem"])
     load.start()
+
+    def fetch(i):
+        v = jnp.where(i < 3, 3 - 3 * xlo, 3 * xlo) + i % 3
+        return pltpu.make_async_copy(coeff.at[:, :, v], s["raw"].at[i % 2], s["raw_sem"].at[i % 2])
+
+    fetch(0).start()
+    fetch(1).start()
+    kron_table(wave, s["kron"])
 
     barrier = pltpu.get_barrier_semaphore()
 
@@ -403,10 +385,6 @@
                 @pl.when(k % 4 == 0)
                 def _():
                     exchange(d, k // 4).wait_recv()
-
-                    @pl.when(k < PIECES - 4 * AHEAD)
-                    def _():
-                        exchange(d, k // 4 + AHEAD).start()
 
                 @pl.when(pos == 0)
                 def _():
@@ -457,26 +435,43 @@
         else:
             pl.when(ok)(act)
 
-    def exchanges(i, _):
-        exchange(0, i).start()
-        exchange(1, i).start()
-        return 0
-
-    lax.fori_loop(0, AHEAD, exchanges, 0)
     load.wait()
     for copy, ok, _ in halo[:2]:
         on(ok, copy.start)
     swap_in(qx, qz)
     for copy, ok, _ in halo[2:]:
         on(ok, copy.start)
-    transpose_in(qx, s["tq"], s["qy"], s["gy"], s["sy"], lambda blk: tick(blk))
+
+    def variable(i, _):
+        half = jnp.where(i < 3, 1 - xlo, xlo)
+        fetch(i).wait()
+
+        def put(c, g, tile):
+            part[half, i % 3, (c + 16 - gz) % 16, g] = tile
+
+        spectral(i, s["raw"], s["rows"], table, s["kron"], s["modes"], s["sums"], put, lambda j: tick((i - 4) * 6 + j))
+
+        @pl.when(i < 4)
+        def _():
+            fetch(i + 2).start()
+
+        @pl.when(i < 3)
+        def _():
+            for h in range(2):
+                for d in range(2):
+                    exchange(d, i * 2 + h).start()
+
+        return 0
+
+    lax.fori_loop(0, 6, variable, 0)
+    transpose_in(qx, s["tq"], s["qy"], s["gy"], s["sy"], lambda blk: tick(blk + 12))
     speed_sweep(s["sy"], s["ay"], 128, 8)
-    face_sweep(s["qy"], s["gy"], s["ay"], s["ty"], 3, 128, 8, 8, lambda i: tick(i + 4))
+    face_sweep(s["qy"], s["gy"], s["ay"], s["ty"], 3, 128, 8, 8, lambda i: tick(i + 16))
     for copy, _, ok in halo[2:]:
         on(ok, copy.wait_recv)
     flux_sweep(qz, s["gz"], s["sz"], 0, 76, 3)
     speed_sweep(s["sz"], s["az"], 32, 16)
-    face_sweep(qz, s["gz"], s["az"], s["tz"], 6, 32, 16, 8, lambda i: tick(i + 52))
+    face_sweep(qz, s["gz"], s["az"], s["tz"], 6, 32, 16, 8, lambda i: tick(i + 64))
     for copy, _, ok in halo[:2]:
         on(ok, copy.wait_recv)
 
@@ -492,7 +487,7 @@
 
     flux_sweep(qx, s["gx"], s["sx"], 0, 88, 1)
     speed_sweep(s["sx"], s["ax"], 16, 32)
-    face_sweep(qx, s["gx"], s["ax"], s["tx"], 6, 16, 32, 16, lambda i: tick(i + 100))
+    face_sweep(qx, s["gx"], s["ax"], s["tx"], 6, 16, 32, 16, lambda i: tick(i + 112))
 
     def strength(x):
         plane = gx * 16 + x
@@ -505,7 +500,7 @@
         tick(n)
         return 0
 
-    lax.fori_loop(124, WIRE_TICKS, drain, 0)
+    lax.fori_loop(136, WIRE_TICKS, drain, 0)
 
     for r in range(2):
 
@@ -546,9 +541,16 @@
 
 
 def local(conserved_fields, coeff, feed_plane):
-    part = spectral(coeff, feed_plane)
+    table, wave = tables(feed_plane)
     scratch = weno_scratch()
     scratch.update(
+        raw=pltpu.VMEM((2, 2, 64, 8, 512), jnp.bfloat16),
+        rows=pltpu.VMEM((512, 1024), jnp.bfloat16),
+        kron=pltpu.VMEM((224, 1024), jnp.bfloat16),
+        modes=pltpu.VMEM((1024, 256), jnp.bfloat16),
+        sums=pltpu.VMEM((224, 512), F32),
+        part=pltpu.VMEM((2, 3, 16, 7, 8, 128), F32),
+        raw_sem=pltpu.SemaphoreType.DMA((2,)),
         land=pltpu.VMEM((3, 16, 7, 8, 128), F32),
         swap=pltpu.VMEM((3, 16, 7, 8, 128), F32),
         feed=pltpu.VMEM((6, 16, 4, 8, 128), F32),
@@ -565,12 +567,12 @@
     out = pl.pallas_call(
         lambda *refs: main_kernel(names, *refs),
         out_shape=jax.ShapeDtypeStruct((6, 512, 128), F32),
-        in_specs=[pl.BlockSpec(memory_space=pl.ANY), pl.BlockSpec(memory_space=pltpu.VMEM)],
+        in_specs=[pl.BlockSpec(memory_space=pl.ANY)] * 2 + [pl.BlockSpec(memory_space=pltpu.VMEM)] * 2,
         out_specs=pl.BlockSpec(memory_space=pltpu.VMEM),
         scratch_shapes=list(scratch.values()),
         compiler_params=pltpu.CompilerParams(collective_id=0, has_side_effects=True, vmem_limit_bytes=56 * 2**20),
         name="section",
-    )(conserved_fields.reshape(6, 512, 128), part.reshape(2, 3, 16, 7, 8, 128))
+    )(conserved_fields.reshape(6, 512, 128), coeff, table, wave)
     return out.reshape(6, 16, 32, 128)
 
 

time: 100 us -> 93.1 us (0.931)
  Pallas kernels: 95.1 us -> 88.8 us
    pallas_call x1 -> x0, Pallas kernels: 18.2 us -> none  [spectral(): pl.pallas_call(spectral_kernel, grid=(4,), out_shape=jax.ShapeDtypeStruct...]
    pallas_call x1, Pallas kernels: 77 us -> 88.8 us  [local(): pl.pallas_call(lambda *refs: main_kernel(names, *refs), out_shape=jax.Sha...]
where the time goes in v3:
time: 93.1 us; the launch traced here: 93 us
  Pallas kernels  88.8 us (95%)
  local copies, waits for them, and re-layouts  3.42 us (4%)
    pallas_call x1, Pallas kernels, local(): pl.pallas_call(lambda *refs: main_kernel(names, *refs), out_shape=jax.Sha...  88.8 us
    unnamed x1, local copies, waits for them, and re-layouts  2.76 us

profile of v3, /device:TPU:1, one launch (start us, length us, event | category | flops | bytes accessed | tf_op | source)
XLA Modules:
  0.0 93.0 jit_solution(18224714526444726690)
XLA Ops:
  0.0 0.7 pad.4
  0.7 0.8 fusion.5.refs_3_
  1.4 88.8 %section.1 = f32[6,512,128]{2,1,0:T(8,128)} custom-call(f32[6,512,128]{2,1,0:T(8,128)} %bitcast.3, bf16[2,64,6,8,512]{4,3,2,1,0:T(8,128)(2,1)} %refs_1_.1, bf16[1024,1024]{1,0:T(8,128)(2,1)} %constant.62.refs_2_, bf16[32,128]{1,0:T(8,128)(2,1)} %fusion.5.refs_3_), custom_call_target="tpu_custom_call" | custom-call | tf_op jit(solution)/shard_map/section/pallas_call | solution.py:567
  90.2 2.8 %copy.6 = f32[6,16,32,128]{3,2,1,0:T(8,128)} copy(f32[6,16,32,128]{3,2,1,0:T(8,128)} %bitcast.2) | data formatting | bytes 3145728
  (4 shorter events, 0.0 us)

commit v4 on v3

--- a/solution.py
+++ b/solution.py
@@ -181,7 +181,7 @@
     lax.fori_loop(0, 32, body, 0)
 
 
-def combine(qx, tx, tz, ty, out, strength):
+def combine(qx, tx, tz, ty, src, out, strength):
     def block(blk, _):
         for c in range(6):
             t = ty[c // 2, pl.ds((c % 2) * 4 + blk, 128, stride=8), :].T
@@ -191,11 +191,15 @@
                 at = pl.ds(pl.multiple_of(x * 32, 32), 32)
                 q = qx[c, pl.ds(pl.multiple_of(96 + x * 32, 32), 32), :]
                 rate = tx[c, at, :] + span + t[k * 32 : k * 32 + 32] + strength(x) * q
+                if c == 5:
+                    rate = rate - src[blk, k * 32 : k * 32 + 32, :]
                 out[c, at, :] = q - 0.05 * rate
         return 0
 
     lax.fori_loop(0, 4, block, 0)
 
+
+def relaxation(qx, src):
     def relax(i, _):
         at = pl.ds(pl.multiple_of(96 + i * 8, 8), 8)
         r, m1, m2, m3, en, ev = [qx[c, at, :] for c in range(6)]
@@ -205,8 +209,7 @@
         temp = p * rinv
         eq = 2.0 / (jnp.exp(2.0 / temp) - 1.0)
         tau = 0.5 * jnp.exp(1.5 * (jnp.exp(jnp.log(temp) * (-1.0 / 3.0)) - 1.0))
-        dst = pl.ds(pl.multiple_of(i * 8, 8), 8)
-        out[5, dst, :] = out[5, dst, :] + 0.05 * ((r * eq - ev) * p / tau)
+        src[i // 16, pl.ds(pl.multiple_of(i % 16 * 8, 8), 8), :] = (r * eq - ev) * p / tau
         return 0
 
     lax.fori_loop(0, 64, relax, 0, unroll=2)
@@ -465,6 +468,7 @@
 
     lax.fori_loop(0, 6, variable, 0)
     transpose_in(qx, s["tq"], s["qy"], s["gy"], s["sy"], lambda blk: tick(blk + 12))
+    relaxation(qx, s["tq"])
     speed_sweep(s["sy"], s["ay"], 128, 8)
     face_sweep(s["qy"], s["gy"], s["ay"], s["ty"], 3, 128, 8, 8, lambda i: tick(i + 16))
     for copy, _, ok in halo[2:]:
@@ -494,7 +498,7 @@
         level = 1.0 - plane.astype(F32) * (1.0 / PLANES)
         return jnp.where(plane < PLANES, 2.0 * level * level, 0.0)
 
-    combine(qx, s["tx"], s["tz"], s["ty"], out, strength)
+    combine(qx, s["tx"], s["tz"], s["ty"], s["tq"], out, strength)
 
     def drain(n, _):
         tick(n)

time: 93.1 us -> 93.7 us (level)
  no operation moved by 1% of the time
where the time goes in v4:
time: 93.7 us; the launch traced here: 93.4 us
  Pallas kernels  89.2 us (95%)
  local copies, waits for them, and re-layouts  3.42 us (4%)
    pallas_call x1, Pallas kernels, local(): pl.pallas_call(lambda *refs: main_kernel(names, *refs), out_shape=jax.Sha...  89.2 us
    unnamed x1, local copies, waits for them, and re-layouts  2.76 us

profile of v4, /device:TPU:1, one launch (start us, length us, event | category | flops | bytes accessed | tf_op | source)
XLA Modules:
  0.0 93.4 jit_solution(2532576831807936619)
XLA Ops:
  0.0 0.7 pad.4
  0.7 0.8 fusion.5.refs_3_
  1.4 89.2 %section.1 = f32[6,512,128]{2,1,0:T(8,128)} custom-call(f32[6,512,128]{2,1,0:T(8,128)} %bitcast.3, bf16[2,64,6,8,512]{4,3,2,1,0:T(8,128)(2,1)} %refs_1_.1, bf16[1024,1024]{1,0:T(8,128)(2,1)} %constant.62.refs_2_, bf16[32,128]{1,0:T(8,128)(2,1)} %fusion.5.refs_3_), custom_call_target="tpu_custom_call" | custom-call | tf_op jit(solution)/shard_map/section/pallas_call | solution.py:571
  90.6 2.8 %copy.6 = f32[6,16,32,128]{3,2,1,0:T(8,128)} copy(f32[6,16,32,128]{3,2,1,0:T(8,128)} %bitcast.2) | data formatting | bytes 3145728
  (4 shorter events, 0.0 us)
